TPU v7x, 512 devices: a whole 4x4x16 slice. The times are simulated.
512 devices in a mesh: vel: 64 (over x_lo, z, core), box: 8 (over x_hi, y).
Axes of the slice: x: 4 (x_hi: 2, x_lo: 2; x = x_hi * 2 + x_lo), y: 4, z: 16, core: 2. Of those that a mesh axis runs over, the one named last changes fastest.
Arguments:
- distribution: float32 [4096, 3, 3, 3, 8, 128], P('vel', None, None, None, 'box'), may hold values from -2.5 to 2.5, as said below
- collision_rate: float32 [8, 128], P('box'), may hold values from 1 to 10
Outputs:
- advanced: float32 [4096, 3, 3, 3, 8, 128], P('vel', None, None, None, 'box')
Inputs may be any that keep to these rules, and one draw needn't show every extreme that they name: `distribution`: coefficient (0,0,0) is positive for every box and velocity; every other coefficient is at most coefficient (0,0,0) of the same box and velocity in magnitude.
All inputs are finite; a program needn't handle non-finite values.
Results may differ from a plain program's by a relative error of at most 0.0003.
Values sent between devices are 32-bit elements; how exact they have to be, the bound alone decides.
No kernel may reach another device: no remote copies, remote signals or barrier semaphores. Data moves between devices by JAX's collectives and lax.ppermute only.
A program may use at most 64 MiB of HBM per device.

v0:
```python
import math

import jax
import jax.numpy as jnp
from jax import lax
from jax.experimental import pallas as pl
from jax.experimental.pallas import tpu as pltpu
from jax.sharding import PartitionSpec as P


NZ = 16
VELS = 64
BOXES = 8
COUNT = 64
STEP = 0.02
SPACING = 0.5
FIRST = -3.75
WEIGHT = SPACING**3
ROWS = 16
TILE = 8
GRANT = 16 << 20


def mode(a, b, c):
    return 9 * a + 3 * b + c


def row_index():
    return lax.broadcasted_iota(jnp.int32, (TILE, 128), 0)


class Place:
    def __init__(self):
        self.vel = lax.axis_index("vel")
        self.box = lax.axis_index("box")
        right = self.vel >= VELS // 2
        self.sx = jnp.where(right, 1.0, -1.0)
        self.wx = (self.vel // 4).astype(jnp.float32) * SPACING + FIRST
        self.ax = self.wx * self.sx
        up = self.vel % 4 >= 2
        self.sy = jnp.where(up, 1.0, -1.0)
        self.first_y = (self.vel % 4 * 4).astype(jnp.float32) * SPACING + FIRST
        self.shift_y = jnp.where(up, NZ, 128 - NZ)
        self.upwind = jnp.where(right, (self.box + BOXES - 1) % BOXES, (self.box + 1) % BOXES)
        self.downwind = jnp.where(right, (self.box + 1) % BOXES, (self.box + BOXES - 1) % BOXES)
        self.lane = lax.broadcasted_iota(jnp.int32, (TILE, 128), 1) % NZ

    def wy(self, j):
        return self.first_y + j.astype(jnp.float32) * SPACING

    def wz(self, half):
        return row_index().astype(jnp.float32) * SPACING + (FIRST + half * TILE * SPACING)

    def from_y(self, values):
        return pltpu.roll(values, self.shift_y, 1)

    def from_z(self, values, half):
        if half:
            return jnp.where(self.lane == 0, pltpu.roll(values, 128 + 1 - NZ, 1), pltpu.roll(values, 1, 1))
        return jnp.where(self.lane == NZ - 1, pltpu.roll(values, NZ - 1, 1), pltpu.roll(values, 127, 1))


def trace(low, middle, high, sign):
    return low + sign * middle + high


def trace_z(low, middle, high, half):
    return low + middle + high if half else low - middle + high


def one_direction(rates, coefs, index, upper, inflow, speed, size):
    _, i1, i2 = index
    jump = inflow - upper
    parts = (
        size * jump,
        (-3.0 * speed) * jump - (6.0 * size) * coefs[i1] - (6.0 * speed) * coefs[i2],
        (5.0 * size) * jump + (10.0 * speed) * coefs[i1],
    )
    for i, part in zip(index, parts):
        rates[i] = part if rates[i] is None else rates[i] + part


def transport(place, coefs, inflow_x, j, half):
    rates = [None] * 27
    for b in range(3):
        for c in range(3):
            index = [mode(a, b, c) for a in range(3)]
            upper = trace(*(coefs[i] for i in index), place.sx)
            one_direction(rates, coefs, index, upper, inflow_x[3 * b + c], place.wx, place.ax)
    wy = place.wy(j)
    ay = wy * place.sy
    for a in range(3):
        for c in range(3):
            index = [mode(a, b, c) for b in range(3)]
            upper = trace(*(coefs[i] for i in index), place.sy)
            one_direction(rates, coefs, index, upper, place.from_y(upper), wy, ay)
    wz = place.wz(half)
    az = wz if half else -wz
    for a in range(3):
        for b in range(3):
            index = [mode(a, b, c) for c in range(3)]
            upper = trace_z(*(coefs[i] for i in index), half)
            one_direction(rates, coefs, index, upper, place.from_z(upper, half), wz, az)
    return rates


def velocity_groups(body):
    def step(j, carry):
        for half in range(2):
            carry = body(j, half, pl.multiple_of((2 * j + half) * TILE, TILE), carry)
        return carry

    return step


def load_coefs(field, start):
    return [field[pl.ds(start * 27 + m, TILE, stride=27), :] for m in range(27)]


def moments(place, j, half, values):
    wy = place.wy(j)
    wz = place.wz(half)
    energy = 0.5 * (place.wx * place.wx + wy * wy + wz * wz)
    return [values, place.wx * values, wy * values, wz * values, energy * values]


def stack_rows(rows):
    index = row_index()
    tile = jnp.zeros((TILE, 128), jnp.float32)
    for i, row in enumerate(rows):
        tile = jnp.where(index == i, jnp.broadcast_to(row, (TILE, 128)), tile)
    return tile


def first_kernel(field, rate, halo, planes):
    place = Place()

    def body(j, half, start, sums):
        coefs = load_coefs(field, start)
        for k in range(9):
            halo[pl.ds(k * COUNT + start, TILE), :] = trace(coefs[k], coefs[9 + k], coefs[18 + k], place.sx)
        base = coefs[0]
        out_x = place.ax * trace(base, coefs[9], coefs[18], place.sx)
        upper_y = trace(base, coefs[3], coefs[6], place.sy)
        upper_z = trace_z(base, coefs[1], coefs[2], half)
        wy = place.wy(j)
        wz = place.wz(half)
        kept = (wy * place.sy) * (place.from_y(upper_y) - upper_y) - out_x
        kept = kept + (wz if half else -wz) * (place.from_z(upper_z, half) - upper_z)
        terms = moments(place, j, half, base) + moments(place, j, half, kept) + moments(place, j, half, out_x)
        return tuple(s + t for s, t in zip(sums, terms))

    zero = jnp.zeros((TILE, 128), jnp.float32)
    sums = lax.fori_loop(0, 4, velocity_groups(body), (zero,) * 15)
    sums = [WEIGHT * jnp.sum(s, axis=0, keepdims=True) for s in sums]
    held = stack_rows(sums[:5] + [rate[...]])
    kept = stack_rows(sums[5:10])
    gone = stack_rows(sums[10:])
    for box in range(BOXES):
        second = jnp.where(place.box == box, kept, jnp.where(place.downwind == box, gone, 0.0))
        for q in range(4):
            first = (q * BOXES + box) * ROWS
            planes[first : first + TILE, :] = held
            planes[first + TILE : first + ROWS, :] = second


def second_kernel(field, rate, halo, planes, middle, halo_out, column, upwind_rate):
    place = Place()
    collision = jnp.broadcast_to(rate[...], (TILE, 128))

    def body(j, half, start, carry):
        coefs = load_coefs(field, start)
        inflow = [halo[pl.ds(k * COUNT + start, TILE), :] for k in range(9)]
        rates = transport(place, coefs, inflow, j, half)
        new = [c + STEP * (r - collision * c) for c, r in zip(coefs, rates)]
        for m in range(27):
            middle[pl.ds(m * COUNT + start, TILE), :] = new[m]
        for k in range(9):
            halo_out[pl.ds(k * COUNT + start, TILE), :] = trace(new[k], new[9 + k], new[18 + k], place.sx)
        return carry

    lax.fori_loop(0, 4, velocity_groups(body), 0)

    def of_box(box):
        return sum(planes[pl.ds(pl.multiple_of((q * BOXES + box) * ROWS, ROWS), TILE), :] for q in range(4))

    own = of_box(place.box)
    upwind = of_box(place.upwind)
    kept = sum(planes[p * ROWS + TILE : (p + 1) * ROWS, :] for p in range(4 * BOXES))
    index = row_index()
    first = jnp.where(index < 5, own, pltpu.roll(upwind, 5, 0))
    second = jnp.where(index < 5, kept, pltpu.roll(upwind, 2, 0))
    for p in range(NZ):
        column[p * ROWS : p * ROWS + TILE, :] = first
        column[p * ROWS + TILE : (p + 1) * ROWS, :] = second
    upwind_rate[...] = planes[pl.ds(place.upwind * ROWS + 5, 1), :]


def states(totals):
    density = totals[0]
    flow = [t / density for t in totals[1:4]]
    square = flow[0] * flow[0] + flow[1] * flow[1] + flow[2] * flow[2]
    temper = (2.0 * totals[4] / density - square) / 3.0
    spread = 2.0 * math.pi * temper
    return flow, density / (spread * jnp.sqrt(spread)), 0.5 / temper


def maxwell_moments(state):
    flow, scale, inverse = state
    centres = lax.broadcasted_iota(jnp.int32, (16, 128), 0).astype(jnp.float32) * SPACING + FIRST
    sums = []
    for u in flow:
        offset = centres - u
        bell = jnp.exp(-(offset * offset) * inverse)
        sums.append([jnp.sum(v, axis=0, keepdims=True) for v in (bell, centres * bell, centres * centres * bell)])
    (x0, x1, x2), (y0, y1, y2), (z0, z1, z2) = sums
    scale = WEIGHT * scale
    energy = x2 * y0 * z0 + x0 * y2 * z0 + x0 * y0 * z2
    return [
        scale * (x0 * y0 * z0),
        scale * (x1 * y0 * z0),
        scale * (x0 * y1 * z0),
        scale * (x0 * y0 * z1),
        scale * (0.5 * energy),
    ]


def third_kernel(field, rate, halo, column, upwind_rate, middle, out):
    place = Place()
    first = sum(column[p * ROWS : p * ROWS + TILE, :] for p in range(NZ))
    second = sum(column[p * ROWS + TILE : (p + 1) * ROWS, :] for p in range(NZ))
    row = lambda tile, i: tile[i : i + 1, :]
    nu = rate[...]
    totals = [row(first, i) for i in range(5)]
    flux = [row(second, i) for i in range(5)]
    upwind = [row(first, 5), row(first, 6), row(first, 7), row(second, 5), row(second, 6)]
    now = states(totals)
    gains = maxwell_moments(now)
    later = states([t + STEP * (f - nu * t + nu * g) for t, f, g in zip(totals, flux, gains)])
    before = states(upwind)

    def spread_out(state, factor):
        flow, scale, inverse = state
        wide = lambda v: jnp.broadcast_to(v, (TILE, 128))
        part = (place.wx - flow[0]) * (place.wx - flow[0])
        return wide(part), wide(flow[1]), wide(flow[2]), wide(factor * scale), wide(-inverse)

    now = spread_out(now, STEP * nu)
    before = spread_out(before, STEP * upwind_rate[...])
    later = spread_out(later, nu)
    collision = jnp.broadcast_to(nu, (TILE, 128))

    def body(j, half, start, carry):
        wy = place.wy(j)
        wz = place.wz(half)

        def bell(state):
            part, flow_y, flow_z, scale, inverse = state
            off_y = wy - flow_y
            off_z = wz - flow_z
            return scale * jnp.exp((part + off_y * off_y + off_z * off_z) * inverse)

        coefs = [middle[pl.ds(m * COUNT + start, TILE), :] for m in range(27)]
        coefs[0] = coefs[0] + bell(now)
        inflow = [halo[pl.ds(k * COUNT + start, TILE), :] for k in range(9)]
        inflow[0] = inflow[0] + bell(before)
        rates = transport(place, coefs, inflow, j, half)
        rates[0] = rates[0] + bell(later)
        for m in range(27):
            here = pl.ds(start * 27 + m, TILE, stride=27)
            moved = coefs[m] + STEP * (rates[m] - collision * coefs[m])
            out[here, :] = 0.5 * field[here, :] + 0.5 * moved
        return carry

    lax.fori_loop(0, 4, velocity_groups(body), 0)


def call(kernel, outs, *args):
    vmem = pl.BlockSpec(memory_space=pltpu.VMEM)
    shapes = [jax.ShapeDtypeStruct(s, jnp.float32) for s in outs]
    moved = sum(4 * math.prod(s) for s in outs) + sum(4 * a.size for a in args)
    return pl.pallas_call(
        kernel,
        out_shape=shapes,
        in_specs=[vmem] * len(args),
        out_specs=[vmem] * len(outs),
        compiler_params=pltpu.CompilerParams(vmem_limit_bytes=GRANT),
        cost_estimate=pl.CostEstimate(flops=4000000, bytes_accessed=moved, transcendentals=30000),
    )(*args)


def downwind_pairs():
    pairs = []
    for vel in range(VELS):
        step = 1 if vel >= VELS // 2 else BOXES - 1
        for box in range(BOXES):
            pairs.append((vel * BOXES + box, vel * BOXES + (box + step) % BOXES))
    return pairs


def vel_of(x, z, core):
    return x * 32 + z * 2 + core


PLANES = [
    [vel_of(x, z, core) * BOXES + box for x in range(2) for core in range(2) for box in range(BOXES)]
    for z in range(NZ)
]
COLUMNS = [[vel_of(x, z, core) for z in range(NZ)] for x in range(2) for core in range(2)]


def exchange(blocks, axis, groups):
    count = len(groups[0])
    blocks = blocks.reshape(count, ROWS, 128)
    blocks = lax.all_to_all(blocks, axis, 0, 0, axis_index_groups=groups)
    return blocks.reshape(count * ROWS, 128)


def step(distribution, collision_rate):
    field = distribution.reshape(COUNT * 27, 128)
    face = (9 * COUNT, 128)
    halo, planes = call(first_kernel, [face, (4 * BOXES * ROWS, 128)], field, collision_rate)
    halo = lax.ppermute(halo, ("vel", "box"), downwind_pairs())
    planes = exchange(planes, ("vel", "box"), PLANES)
    middle, halo, column, upwind_rate = call(
        second_kernel,
        [(27 * COUNT, 128), face, (NZ * ROWS, 128), (1, 128)],
        field,
        collision_rate,
        halo,
        planes,
    )
    halo = lax.ppermute(halo, ("vel", "box"), downwind_pairs())
    column = exchange(column, "vel", COLUMNS)
    (out,) = call(
        third_kernel, [(COUNT * 27, 128)], field, collision_rate, halo, column, upwind_rate, middle
    )
    return out.reshape(distribution.shape)


def solution(mesh):
    return jax.shard_map(
        step,
        mesh=mesh,
        in_specs=(P("vel", None, None, None, "box", None), P("box", None)),
        out_specs=P("vel", None, None, None, "box", None),
        check_vma=False,
    )
```

profile of v0, /device:TPU:32, one launch (start us, length us, event | category | flops | bytes accessed | tf_op | source)
XLA Modules:
  0.0 54.0 jit_solution(50052175502794543)
XLA Ops:
  0.0 0.0 copy-start.2
  0.0 0.7 %copy-done.2 = f32[1,128]{1,0:T(1,128)S(1)} copy-done((f32[1,128]{1,0:T(1,128)S(1)}, f32[1,128]{1,0:T(1,128)}, u32[]{:S(2)}) %copy-start.2) | copy-done | bytes 536
  0.7 0.0 copy-start
  0.7 1.2 %copy-done = f32[64,3,3,3,1,128]{5,4,3,2,1,0:T(1,128)S(1)} copy-done((f32[64,3,3,3,1,128]{5,4,3,2,1,0:T(1,128)S(1)}, f32[64,3,3,3,1,128]{5,4,3,2,1,0:T(1,128)}, u32[]{:S(2)}) %copy-start) | copy-done | bytes 884760
  1.8 0.4 shard_map.28
  2.2 7.4 %collective-permute-start = (f32[576,128]{1,0:T(8,128)S(1)}, f32[576,128]{1,0:T(8,128)S(1)}, u32[]{:S(2)}, u32[]{:S(2)}) collective-permute-start(f32[576,128]{1,0:T(8,128)S(1)} %get-tuple-element.11), channel_id=1, source_target_pairs={{0,7},{1,0},{2,1},{3,2},{4,3},{5,4},{6,5},{7,6},{8,15},{9,8},{10,9... | collective-permute-start | bytes 884744 | tf_op jit(solution)/shard_map/ppermute | solution.py:323
  9.6 12.3 %all_to_all.10 = f32[32,16,128]{2,1,0:T(8,128)S(1)} all-to-all(f32[32,16,128]{2,1,0:T(8,128)S(1)} %bitcast.11), channel_id=1, replica_groups={{0,1,2,3,4,5,6,7,8,9,10,11,12,13,14,15,256,257,258,259,260,261,262,263,..., dimensions={0} | all-to-all | bytes 524288 | tf_op jit(solution)/shard_map/all_to_all | solution.py:315
  21.9 0.0 copy-start.1
  22.0 0.0 collective-permute-done.halo
  22.0 1.4 %shard_map.29 = (f32[1728,128]{1,0:T(8,128)S(1)}, f32[576,128]{1,0:T(8,128)S(1)}, f32[256,128]{1,0:T(8,128)}, f32[1,128]{1,0:T(1,128)S(1)}) custom-call(f32[1728,128]{1,0:T(8,128)S(1)} %bitcast.7, f32[1,128]{1,0:T(1,128)S(1)} %copy-done.2, f32[576,128]{1,0:T(8,128)S(1)} %collective-permute-done.halo, f32[512,128]{1,0:T(8,128)S(1)} %bitcast.9), custom_call_target="tpu_custom_call" | custom-call | flops 4000000 | bytes 2753536 | tf_op jit(solution)/shard_map/pallas_call | solution.py:282
  23.4 15.2 %all-to-all-start.1 = ((f32[16,16,128]{2,1,0:T(8,128)}), f32[16,16,128]{2,1,0:T(8,128)S(1)}, u32[]{:S(2)}, u32[]{:S(2)}) async-start(f32[16,16,128]{2,1,0:T(8,128)} %bitcast.3), calls=%async_computation.1 | async-start | bytes 262144 | tf_op jit(solution)/shard_map/all_to_all | solution.py:315
  38.6 4.7 %collective-permute-start.1 = (f32[576,128]{1,0:T(8,128)S(1)}, f32[576,128]{1,0:T(8,128)S(1)}, u32[]{:S(2)}, u32[]{:S(2)}) collective-permute-start(f32[576,128]{1,0:T(8,128)S(1)} %get-tuple-element.13), channel_id=1, source_target_pairs={{0,7},{1,0},{2,1},{3,2},{4,3},{5,4},{6,5},{7,6},{8,15},{9,8},{10,9... | collective-permute-start | bytes 884744 | tf_op jit(solution)/shard_map/ppermute | solution.py:333
  43.3 5.9 %collective-permute-done.1.halo = f32[576,128]{1,0:T(8,128)S(1)} collective-permute-done((f32[576,128]{1,0:T(8,128)S(1)}, f32[576,128]{1,0:T(8,128)S(1)}, u32[]{:S(2)}, u32[]{:S(2)}) %collective-permute-start.1) | collective-permute-done | bytes 294944 | tf_op jit(solution)/shard_map/ppermute | solution.py:333
  49.2 2.9 %all-to-all-done.1 = f32[16,16,128]{2,1,0:T(8,128)S(1)} async-done(((f32[16,16,128]{2,1,0:T(8,128)}), f32[16,16,128]{2,1,0:T(8,128)S(1)}, u32[]{:S(2)}, u32[]{:S(2)}) %all-to-all-start.1) | async-done | bytes 131104 | tf_op jit(solution)/shard_map/all_to_all | solution.py:315
  52.1 0.0 copy-done.1
  52.1 1.9 %shard_map.30 = f32[1728,128]{1,0:T(8,128)} custom-call(f32[1728,128]{1,0:T(8,128)S(1)} %bitcast.8, f32[1,128]{1,0:T(1,128)S(1)} %copy-done.2, f32[576,128]{1,0:T(8,128)S(1)} %collective-permute-done.1.halo, f32[256,128]{1,0:T(8,128)S(1)} %bitcast.10, f32[1,128]{1,0:T(1,128)S(1)} %get-tuple-element.15.upwind_rate, f32[1728,128]{1,0:T(8,128)S(1)} %get-tuple-element.16.middle), custom_call_target="tpu_custom_call" | custom-call | flops 4000000 | bytes 3081216 | tf_op jit(solution)/shard_map/pallas_call | solution.py:282
Async XLA Ops:
  0.0 0.7 %copy-start.2 = (f32[1,128]{1,0:T(1,128)S(1)}, f32[1,128]{1,0:T(1,128)}, u32[]{:S(2)}) copy-start(f32[1,128]{1,0:T(1,128)} %rate.5) | copy-start | bytes 1540
  0.7 1.2 %copy-start = (f32[64,3,3,3,1,128]{5,4,3,2,1,0:T(1,128)S(1)}, f32[64,3,3,3,1,128]{5,4,3,2,1,0:T(1,128)}, u32[]{:S(2)}) copy-start(f32[64,3,3,3,1,128]{5,4,3,2,1,0:T(1,128)} %param.2) | copy-start | bytes 2654212
  2.2 19.7 %collective-permute-start = (f32[576,128]{1,0:T(8,128)S(1)}, f32[576,128]{1,0:T(8,128)S(1)}, u32[]{:S(2)}, u32[]{:S(2)}) collective-permute-start(f32[576,128]{1,0:T(8,128)S(1)} %get-tuple-element.11), channel_id=1, source_target_pairs={{0,7},{1,0},{2,1},{3,2},{4,3},{5,4},{6,5},{7,6},{8,15},{9,8},{10,9... | collective-permute-start | bytes 884744 | tf_op jit(solution)/shard_map/ppermute | solution.py:323
  21.9 30.2 %copy-start.1 = (f32[64,3,3,3,1,128]{5,4,3,2,1,0:T(1,128)S(1)}, f32[64,3,3,3,1,128]{5,4,3,2,1,0:T(1,128)}, u32[]{:S(2)}) copy-start(f32[64,3,3,3,1,128]{5,4,3,2,1,0:T(1,128)} %param.2) | copy-start | bytes 2654212
  23.4 28.7 %all-to-all-start.1 = ((f32[16,16,128]{2,1,0:T(8,128)}), f32[16,16,128]{2,1,0:T(8,128)S(1)}, u32[]{:S(2)}, u32[]{:S(2)}) async-start(f32[16,16,128]{2,1,0:T(8,128)} %bitcast.3), calls=%async_computation.1 | async-start | bytes 262144 | tf_op jit(solution)/shard_map/all_to_all | solution.py:315
  38.6 10.6 %collective-permute-start.1 = (f32[576,128]{1,0:T(8,128)S(1)}, f32[576,128]{1,0:T(8,128)S(1)}, u32[]{:S(2)}, u32[]{:S(2)}) collective-permute-start(f32[576,128]{1,0:T(8,128)S(1)} %get-tuple-element.13), channel_id=1, source_target_pairs={{0,7},{1,0},{2,1},{3,2},{4,3},{5,4},{6,5},{7,6},{8,15},{9,8},{10,9... | collective-permute-start | bytes 884744 | tf_op jit(solution)/shard_map/ppermute | solution.py:333
where the time goes:
time: 54.3 us; the launch traced here: 54 us
  starting transfers between devices  27.3 us (50%)
  blocking collectives  12.3 us (23%)
  waiting for transfers between devices  8.83 us (16%)
  Pallas kernels  3.7 us (7%)
  local copies, waits for them, and re-layouts  1.83 us (3%)
    all_to_all x1, starting transfers between devices, exchange(): blocks = lax.all_to_all(blocks, axis, 0, 0, axis_index_groups=groups)  15.2 us
    all_to_all x1, blocking collectives, exchange(): blocks = lax.all_to_all(blocks, axis, 0, 0, axis_index_groups=groups)  12.3 us
    ppermute x2, starting transfers between devices, step(): halo = lax.ppermute(halo, ('vel', 'box'), downwind_pairs())  12.1 us
    ppermute x2, waiting for transfers between devices, step(): halo = lax.ppermute(halo, ('vel', 'box'), downwind_pairs())  5.92 us
    pallas_call x3, Pallas kernels, call(): pl.pallas_call(kernel, out_shape=shapes, in_specs=[vmem] * len(args), out...  3.7 us
    all_to_all x1, waiting for transfers between devices, exchange(): blocks = lax.all_to_all(blocks, axis, 0, 0, axis_index_groups=groups)  2.91 us
    unnamed x6, local copies, waits for them, and re-layouts  1.83 us
  transfers between devices with their start and end apart: 3, of which 2 were waited for; matrix products, arithmetic and copies ran while one was open for 0% of the time, Pallas kernels for 0%

commit v1 on v0

--- a/solution.py
+++ b/solution.py
@@ -19,6 +19,7 @@
 ROWS = 16
 TILE = 8
 GRANT = 16 << 20
+CHUNK = COUNT * 27 // 4
 
 
 def mode(a, b, c):
@@ -132,10 +133,21 @@
     return tile
 
 
-def first_kernel(field, rate, halo, planes):
+def chunk_copy(source, target, sems, j):
+    rows = pl.ds(pl.multiple_of(j * CHUNK, CHUNK), CHUNK)
+    return pltpu.make_async_copy(source.at[rows], target.at[rows], sems.at[j])
+
+
+def first_kernel(field_hbm, rate_hbm, halo, planes, field, rate, sems):
     place = Place()
+    for j in range(4):
+        chunk_copy(field_hbm, field, sems, j).start()
+    rate_copy = pltpu.make_async_copy(rate_hbm, rate, sems.at[4])
+    rate_copy.start()
 
     def body(j, half, start, sums):
+        if not half:
+            chunk_copy(field_hbm, field, sems, j).wait()
         coefs = load_coefs(field, start)
         for k in range(9):
             halo[pl.ds(k * COUNT + start, TILE), :] = trace(coefs[k], coefs[9 + k], coefs[18 + k], place.sx)
@@ -152,6 +164,7 @@
 
     zero = jnp.zeros((TILE, 128), jnp.float32)
     sums = lax.fori_loop(0, 4, velocity_groups(body), (zero,) * 15)
+    rate_copy.wait()
     sums = [WEIGHT * jnp.sum(s, axis=0, keepdims=True) for s in sums]
     held = stack_rows(sums[:5] + [rate[...]])
     kept = stack_rows(sums[5:10])
@@ -225,7 +238,7 @@
     ]
 
 
-def third_kernel(field, rate, halo, column, upwind_rate, middle, out):
+def third_kernel(field, rate, halo, column, upwind_rate, middle, out_hbm, out, sems):
     place = Place()
     first = sum(column[p * ROWS : p * ROWS + TILE, :] for p in range(NZ))
     second = sum(column[p * ROWS + TILE : (p + 1) * ROWS, :] for p in range(NZ))
@@ -270,20 +283,26 @@
             here = pl.ds(start * 27 + m, TILE, stride=27)
             moved = coefs[m] + STEP * (rates[m] - collision * coefs[m])
             out[here, :] = 0.5 * field[here, :] + 0.5 * moved
+        if half:
+            chunk_copy(out, out_hbm, sems, j).start()
         return carry
 
     lax.fori_loop(0, 4, velocity_groups(body), 0)
-
-
-def call(kernel, outs, *args):
+    for j in range(4):
+        chunk_copy(out, out_hbm, sems, j).wait()
+
+
+def call(kernel, outs, *args, remote_in=0, remote_out=False, scratch=()):
     vmem = pl.BlockSpec(memory_space=pltpu.VMEM)
+    hbm = pl.BlockSpec(memory_space=pltpu.HBM)
     shapes = [jax.ShapeDtypeStruct(s, jnp.float32) for s in outs]
     moved = sum(4 * math.prod(s) for s in outs) + sum(4 * a.size for a in args)
     return pl.pallas_call(
         kernel,
         out_shape=shapes,
-        in_specs=[vmem] * len(args),
-        out_specs=[vmem] * len(outs),
+        in_specs=[hbm] * remote_in + [vmem] * (len(args) - remote_in),
+        out_specs=[hbm if remote_out else vmem] * len(outs),
+        scratch_shapes=scratch,
         compiler_params=pltpu.CompilerParams(vmem_limit_bytes=GRANT),
         cost_estimate=pl.CostEstimate(flops=4000000, bytes_accessed=moved, transcendentals=30000),
     )(*args)
@@ -317,23 +336,41 @@
 
 
 def step(distribution, collision_rate):
-    field = distribution.reshape(COUNT * 27, 128)
+    field = pltpu.with_memory_space_constraint(distribution.reshape(COUNT * 27, 128), pltpu.HBM)
+    collision_rate = pltpu.with_memory_space_constraint(collision_rate, pltpu.HBM)
     face = (9 * COUNT, 128)
-    halo, planes = call(first_kernel, [face, (4 * BOXES * ROWS, 128)], field, collision_rate)
+    whole = (27 * COUNT, 128)
+    halo, planes, field, rate = call(
+        first_kernel,
+        [face, (4 * BOXES * ROWS, 128), whole, (1, 128)],
+        field,
+        collision_rate,
+        remote_in=2,
+        scratch=[pltpu.SemaphoreType.DMA((5,))],
+    )
     halo = lax.ppermute(halo, ("vel", "box"), downwind_pairs())
     planes = exchange(planes, ("vel", "box"), PLANES)
     middle, halo, column, upwind_rate = call(
         second_kernel,
-        [(27 * COUNT, 128), face, (NZ * ROWS, 128), (1, 128)],
+        [whole, face, (NZ * ROWS, 128), (1, 128)],
         field,
-        collision_rate,
+        rate,
         halo,
         planes,
     )
     halo = lax.ppermute(halo, ("vel", "box"), downwind_pairs())
     column = exchange(column, "vel", COLUMNS)
     (out,) = call(
-        third_kernel, [(COUNT * 27, 128)], field, collision_rate, halo, column, upwind_rate, middle
+        third_kernel,
+        [whole],
+        field,
+        rate,
+        halo,
+        column,
+        upwind_rate,
+        middle,
+        remote_out=True,
+        scratch=[pltpu.VMEM(whole, jnp.float32), pltpu.SemaphoreType.DMA((4,))],
     )
     return out.reshape(distribution.shape)
 

time: 54.3 us -> 53.3 us (0.982)
  local copies, waits for them, and re-layouts: 1.83 us -> 0 us
  Pallas kernels: 3.7 us -> 4.52 us
    unnamed x6 -> x0, local copies, waits for them, and re-layouts: 1.83 us -> none
    pallas_call x3, Pallas kernels: 3.7 us -> 4.52 us  [call(): pl.pallas_call(kernel, out_shape=shapes, in_specs=[hbm] * remote_in + [vm...]
where the time goes in v1:
time: 53.3 us; the launch traced here: 53 us
  starting transfers between devices  27.3 us (51%)
  blocking collectives  12.3 us (23%)
  waiting for transfers between devices  8.83 us (17%)
  Pallas kernels  4.52 us (8%)
    all_to_all x1, starting transfers between devices, exchange(): blocks = lax.all_to_all(blocks, axis, 0, 0, axis_index_groups=groups)  15.2 us
    all_to_all x1, blocking collectives, exchange(): blocks = lax.all_to_all(blocks, axis, 0, 0, axis_index_groups=groups)  12.3 us
    ppermute x2, starting transfers between devices, step(): halo = lax.ppermute(halo, ('vel', 'box'), downwind_pairs())  12.1 us
    ppermute x2, waiting for transfers between devices, step(): halo = lax.ppermute(halo, ('vel', 'box'), downwind_pairs())  5.92 us
    pallas_call x3, Pallas kernels, call(): pl.pallas_call(kernel, out_shape=shapes, in_specs=[hbm] * remote_in + [vm...  4.52 us
    all_to_all x1, waiting for transfers between devices, exchange(): blocks = lax.all_to_all(blocks, axis, 0, 0, axis_index_groups=groups)  2.91 us
  transfers between devices with their start and end apart: 3, of which 2 were waited for; matrix products, arithmetic and copies ran while one was open for 0% of the time, Pallas kernels for 0%

profile of v1, /device:TPU:32, one launch (start us, length us, event | category | flops | bytes accessed | tf_op | source)
XLA Modules:
  0.0 53.0 jit_solution(17430913287236618275)
XLA Ops:
  0.0 1.4 %shard_map.28 = (f32[576,128]{1,0:T(8,128)S(1)}, f32[512,128]{1,0:T(8,128)S(1)}, f32[1728,128]{1,0:T(8,128)S(1)}, f32[1,128]{1,0:T(1,128)S(1)}) custom-call(f32[1728,128]{1,0:T(8,128)} %bitcast.9, f32[1,128]{1,0:T(1,128)} %rate_hbm.1), custom_call_target="tpu_custom_call" | custom-call | flops 4000000 | bytes 2327552 | tf_op jit(solution)/shard_map/pallas_call | solution.py:300
  1.4 7.4 %collective-permute-start = (f32[576,128]{1,0:T(8,128)S(1)}, f32[576,128]{1,0:T(8,128)S(1)}, u32[]{:S(2)}, u32[]{:S(2)}) collective-permute-start(f32[576,128]{1,0:T(8,128)S(1)} %get-tuple-element.15), channel_id=1, source_target_pairs={{0,7},{1,0},{2,1},{3,2},{4,3},{5,4},{6,5},{7,6},{8,15},{9,8},{10,9... | collective-permute-start | bytes 884744 | tf_op jit(solution)/shard_map/ppermute | solution.py:351
  8.8 12.3 %all_to_all.10 = f32[32,16,128]{2,1,0:T(8,128)S(1)} all-to-all(f32[32,16,128]{2,1,0:T(8,128)S(1)} %bitcast.8), channel_id=1, replica_groups={{0,1,2,3,4,5,6,7,8,9,10,11,12,13,14,15,256,257,258,259,260,261,262,263,..., dimensions={0} | all-to-all | bytes 524288 | tf_op jit(solution)/shard_map/all_to_all | solution.py:334
  21.2 0.0 collective-permute-done.halo
  21.2 1.4 %shard_map.29 = (f32[1728,128]{1,0:T(8,128)S(1)}, f32[576,128]{1,0:T(8,128)S(1)}, f32[256,128]{1,0:T(8,128)}, f32[1,128]{1,0:T(1,128)S(1)}) custom-call(f32[1728,128]{1,0:T(8,128)S(1)} %get-tuple-element.13.field, f32[1,128]{1,0:T(1,128)S(1)} %get-tuple-element.14.rate, f32[576,128]{1,0:T(8,128)S(1)} %collective-permute-done.halo, f32[512,128]{1,0:T(8,128)S(1)} %bitcast.6), custom_call_target="tpu_custom_call" | custom-call | flops 4000000 | bytes 2753536 | tf_op jit(solution)/shard_map/pallas_call | solution.py:300
  22.6 15.2 %all-to-all-start.1 = ((f32[16,16,128]{2,1,0:T(8,128)}), f32[16,16,128]{2,1,0:T(8,128)S(1)}, u32[]{:S(2)}, u32[]{:S(2)}) async-start(f32[16,16,128]{2,1,0:T(8,128)} %bitcast.3), calls=%async_computation.1 | async-start | bytes 262144 | tf_op jit(solution)/shard_map/all_to_all | solution.py:334
  37.8 4.7 %collective-permute-start.1 = (f32[576,128]{1,0:T(8,128)S(1)}, f32[576,128]{1,0:T(8,128)S(1)}, u32[]{:S(2)}, u32[]{:S(2)}) collective-permute-start(f32[576,128]{1,0:T(8,128)S(1)} %get-tuple-element.17), channel_id=1, source_target_pairs={{0,7},{1,0},{2,1},{3,2},{4,3},{5,4},{6,5},{7,6},{8,15},{9,8},{10,9... | collective-permute-start | bytes 884744 | tf_op jit(solution)/shard_map/ppermute | solution.py:361
  42.5 5.9 %collective-permute-done.1.halo = f32[576,128]{1,0:T(8,128)S(1)} collective-permute-done((f32[576,128]{1,0:T(8,128)S(1)}, f32[576,128]{1,0:T(8,128)S(1)}, u32[]{:S(2)}, u32[]{:S(2)}) %collective-permute-start.1) | collective-permute-done | bytes 294944 | tf_op jit(solution)/shard_map/ppermute | solution.py:361
  48.4 2.9 %all-to-all-done.1 = f32[16,16,128]{2,1,0:T(8,128)S(1)} async-done(((f32[16,16,128]{2,1,0:T(8,128)}), f32[16,16,128]{2,1,0:T(8,128)S(1)}, u32[]{:S(2)}, u32[]{:S(2)}) %all-to-all-start.1) | async-done | bytes 131104 | tf_op jit(solution)/shard_map/all_to_all | solution.py:334
  51.3 1.7 %shard_map.30 = f32[1728,128]{1,0:T(8,128)} custom-call(f32[1728,128]{1,0:T(8,128)S(1)} %get-tuple-element.13.field, f32[1,128]{1,0:T(1,128)S(1)} %get-tuple-element.14.rate, f32[576,128]{1,0:T(8,128)S(1)} %collective-permute-done.1.halo, f32[256,128]{1,0:T(8,128)S(1)} %bitcast.7, f32[1,128]{1,0:T(1,128)S(1)} %get-tuple-element.19.upwind_rate, ...), custom_call_target="tpu_custom_call" | custom-call | flops 4000000 | bytes 3081216 | tf_op jit(solution)/shard_map/pallas_call | solution.py:300
Async XLA Ops:
  1.4 19.7 %collective-permute-start = (f32[576,128]{1,0:T(8,128)S(1)}, f32[576,128]{1,0:T(8,128)S(1)}, u32[]{:S(2)}, u32[]{:S(2)}) collective-permute-start(f32[576,128]{1,0:T(8,128)S(1)} %get-tuple-element.15), channel_id=1, source_target_pairs={{0,7},{1,0},{2,1},{3,2},{4,3},{5,4},{6,5},{7,6},{8,15},{9,8},{10,9... | collective-permute-start | bytes 884744 | tf_op jit(solution)/shard_map/ppermute | solution.py:351
  22.6 28.7 %all-to-all-start.1 = ((f32[16,16,128]{2,1,0:T(8,128)}), f32[16,16,128]{2,1,0:T(8,128)S(1)}, u32[]{:S(2)}, u32[]{:S(2)}) async-start(f32[16,16,128]{2,1,0:T(8,128)} %bitcast.3), calls=%async_computation.1 | async-start | bytes 262144 | tf_op jit(solution)/shard_map/all_to_all | solution.py:334
  37.8 10.6 %collective-permute-start.1 = (f32[576,128]{1,0:T(8,128)S(1)}, f32[576,128]{1,0:T(8,128)S(1)}, u32[]{:S(2)}, u32[]{:S(2)}) collective-permute-start(f32[576,128]{1,0:T(8,128)S(1)} %get-tuple-element.17), channel_id=1, source_target_pairs={{0,7},{1,0},{2,1},{3,2},{4,3},{5,4},{6,5},{7,6},{8,15},{9,8},{10,9... | collective-permute-start | bytes 884744 | tf_op jit(solution)/shard_map/ppermute | solution.py:361
